TPU v7x, 32 devices: a whole 2x2x4 slice. The times are simulated.
32 devices in a mesh: tm: 8 (over z, y), order: 4 (over x, core).
Axes of the slice: x: 2, y: 2, z: 4, core: 2. Of those that a mesh axis runs over, the one named last changes fastest.
Arguments:
- design: bfloat16 [3, 1024, 65536], P(None, 'tm', 'order'), may hold values from -0.109375 to 0.109375
- gap_flags: int32 [1024], P('tm'), may hold values 0 or 1
- segment_ids: int32 [1024], P('tm'), may hold values from 0 to 3, never falling along the last dimension, each value on 1 to 512 neighbouring positions
- ar_order: int32 [3], replicated, may hold values from 1 to 4
- ma_order: int32 [3], replicated, may hold values from 1 to 4
- ar_roots: float32 [3, 4], replicated, may hold values from -0.5 to 1, as said below
- ma_roots: float32 [3, 4], replicated, may hold values from -0.5 to 1, as said below
- kaula: float32 [4, 16384], P('order', 'tm'), may hold values from 0.2 to 2
- precond: float32 [4, 128, 128, 128], P('order', 'tm'), as said below
- solution: float32 [16, 4, 16384], P(None, 'order', 'tm'), may hold values from -6 to 6
- residual: float32 [16, 4, 16384], P(None, 'order', 'tm'), may hold values from -6 to 6
- direction: float32 [16, 4, 16384], P(None, 'order', 'tm'), may hold values from -6 to 6
Outputs:
- new_solution: float32 [16, 4, 16384], P(None, 'order', 'tm')
- new_residual: float32 [16, 4, 16384], P(None, 'order', 'tm')
- new_direction: float32 [16, 4, 16384], P(None, 'order', 'tm')
Inputs may be any that keep to these rules, and one draw needn't show every extreme that they name: The first root of each component of ar_roots lies within 2 / 1024 below 1; the others lie within 0.5 of zero. The first root of each component of ma_roots lies within 12 / 1024 below 1; the others lie within 0.5 of zero. `precond`: every block is symmetric positive definite.
All inputs are finite; a program needn't handle non-finite values. No bound on the sum of `gap_flags` on one device may be relied on, other than what follows from the above.
Results may differ from a plain program's by a relative error of at most 0.0036.
Values may be sent and summed in bfloat16 or wider, within the bound.
A program may use at most 64 MiB of HBM per device.

v0:
```python
import jax
import jax.numpy as jnp
from jax import lax
from jax.sharding import PartitionSpec as P

PMAX = 4
QMAX = 4


precise = lax.Precision.HIGHEST


def extended_2(block, sides, width):
    for axis, dim in sides:
        count = lax.axis_size(axis)
        forward = [(i, i + 1) for i in range(count - 1)]
        backward = [(target, source) for source, target in forward]
        low = lax.ppermute(
            lax.slice_in_dim(block, block.shape[dim] - width, None, axis=dim), axis, forward
        )
        high = lax.ppermute(lax.slice_in_dim(block, 0, width, axis=dim), axis, backward)
        block = jnp.concatenate([low, block, high], axis=dim)
    return block


def shifted(block, axis, distance):
    devices = range(lax.axis_size(axis))
    route = [(i - distance, i) for i in devices if i - distance in devices]
    return lax.ppermute(block, axis, route)


def entering(value, axis, combine, identity, reverse):
    size, place = (lax.axis_size(axis), lax.axis_index(axis))
    everything = jax.tree.map(lambda part: lax.all_gather(part, axis), value)
    start = jax.tree.map(
        lambda part, zero: jnp.broadcast_to(jnp.asarray(zero, part.dtype), part.shape),
        value,
        identity,
    )

    def step(k, before):
        at = size - 1 - k if reverse else k
        reached = at > place if reverse else at < place
        new = combine(before, jax.tree.map(lambda part: part[at], everything))
        return jax.tree.map(lambda a, b: jnp.where(reached, a, b), new, before)

    return lax.fori_loop(0, size, step, start)


def polynomial(root_values, filter_order):
    number_roots = root_values.shape[1]
    coeffs = jnp.concatenate(
        [jnp.ones((3, 1), jnp.float32), jnp.zeros((3, number_roots), jnp.float32)], axis=1
    )
    for position in range(number_roots):
        active = jnp.where(
            position < filter_order,
            root_values[:, position],
            jnp.zeros_like(root_values[:, position]),
        )
        lagged = jnp.concatenate([jnp.zeros_like(coeffs[:, :1]), coeffs[:, :-1]], axis=1)
        coeffs = coeffs - active[:, None] * lagged
    return coeffs


def same_ids(left_ids, right_ids):
    return jnp.where(left_ids == right_ids, 1.0, 0.0).astype(jnp.float32)


def chain_combine(earlier, later):
    first_maps, first_shift = earlier
    second_maps, second_shift = later
    joined_maps = jnp.einsum("cij,cjk->cik", second_maps, first_maps, precision=precise)
    joined_shift = (
        jnp.einsum("cij,rcj->rci", second_maps, first_shift, precision=precise) + second_shift
    )
    return (joined_maps, joined_shift)


def on_device(
    design,
    gap_flags,
    segment_ids,
    ar_order,
    ma_order,
    ar_roots,
    ma_roots,
    kaula,
    precond,
    solution,
    residual,
    direction,
):
    epochs = segment_ids.shape[0]
    columns = design.shape[2]
    share_len = direction.shape[2]
    rhs_count = direction.shape[0]
    ar_coeffs = polynomial(ar_roots, ar_order)
    ma_coeffs = polynomial(ma_roots, ma_order)
    rim_ids = extended_2(segment_ids + 1, (("tm", 0),), PMAX)
    local_ids = rim_ids[PMAX : PMAX + epochs]
    row_grid = lax.broadcasted_iota(jnp.int32, (epochs, epochs), 0)
    col_grid = lax.broadcasted_iota(jnp.int32, (epochs, epochs), 1)
    pair_same = same_ids(local_ids[:, None], local_ids[None, :])
    identity = jnp.eye(epochs, dtype=jnp.float32)
    lower = jnp.broadcast_to(identity, (3, epochs, epochs))
    time_grid = lax.broadcasted_iota(jnp.int32, (epochs, PMAX), 0)
    state_grid = lax.broadcasted_iota(jnp.int32, (epochs, PMAX), 1)
    same_before = same_ids(local_ids[:, None], rim_ids[:PMAX][::-1][None, :])
    same_after = same_ids(local_ids[:, None], rim_ids[PMAX + epochs :][None, :])
    enter_before = jnp.zeros((3, epochs, PMAX), jnp.float32)
    enter_after = jnp.zeros((3, epochs, PMAX), jnp.float32)
    for lag_step in range(1, PMAX + 1):
        lag_weight = ar_coeffs[:, lag_step][:, None, None]
        lower = (
            lower + lag_weight * jnp.where(row_grid - col_grid == lag_step, pair_same, 0.0)[None]
        )
        enter_before = (
            enter_before
            + lag_weight * jnp.where(time_grid + 1 + state_grid == lag_step, same_before, 0.0)[None]
        )
        enter_after = (
            enter_after
            + lag_weight
            * jnp.where(epochs + state_grid - time_grid == lag_step, same_after, 0.0)[None]
        )
    inverse = jax.scipy.linalg.solve_triangular(
        lower, jnp.broadcast_to(identity, (3, epochs, epochs)), lower=True
    )
    from_before = -jnp.einsum("cts,csm->ctm", inverse, enter_before, precision=precise)
    from_after = -jnp.einsum("cst,csm->ctm", inverse, enter_after, precision=precise)
    gaps = gap_flags.astype(jnp.float32)
    ident_maps = jnp.broadcast_to(jnp.eye(PMAX, dtype=jnp.float32), (3, PMAX, PMAX))
    packed = direction.astype(jnp.bfloat16)
    design_flat = design.reshape(3 * epochs, columns)
    partial_obs = lax.dot_general(
        lax.all_gather(packed, "tm", axis=2, tiled=True)[:, 0, :],
        design_flat,
        (((1,), (1,)), ((), ())),
        preferred_element_type=jnp.float32,
    )
    partial_obs = partial_obs.reshape(rhs_count, 3, epochs)
    whole_obs = lax.psum(partial_obs, "order")
    masked = whole_obs * gaps[None, None, :]
    before_vals = shifted(masked[:, :, epochs - QMAX :], "tm", 1)
    extended = jnp.concatenate([before_vals, masked], axis=2)
    moving = jnp.zeros_like(masked)
    for lag_step in range(QMAX + 1):
        joined = same_ids(rim_ids[PMAX - lag_step : PMAX - lag_step + epochs], local_ids)
        moving = (
            moving
            + ma_coeffs[:, lag_step][None, :, None]
            * extended[:, :, QMAX - lag_step : QMAX - lag_step + epochs]
            * joined[None, None, :]
        )
    local_fwd = jnp.einsum("cts,rcs->rct", inverse, moving, precision=precise)
    fwd_maps = from_before[:, ::-1, :][:, :PMAX, :]
    fwd_shift = local_fwd[:, :, ::-1][:, :, :PMAX]
    ident_shift = jnp.zeros_like(fwd_shift)
    _, state_in = entering(
        (fwd_maps, fwd_shift), "tm", chain_combine, (ident_maps, ident_shift), False
    )
    filtered = local_fwd + jnp.einsum("ctm,rcm->rct", from_before, state_in, precision=precise)
    local_back = jnp.einsum("cst,rcs->rct", inverse, filtered, precision=precise)
    _, state_back = entering(
        (from_after[:, :PMAX, :], local_back[:, :, :PMAX]),
        "tm",
        chain_combine,
        (ident_maps, ident_shift),
        True,
    )
    adjoint = local_back + jnp.einsum("ctm,rcm->rct", from_after, state_back, precision=precise)
    after_vals = shifted(adjoint[:, :, :QMAX], "tm", -1)
    extended_back = jnp.concatenate([adjoint, after_vals], axis=2)
    moved_back = jnp.zeros_like(adjoint)
    for lag_step in range(QMAX + 1):
        joined = same_ids(local_ids, rim_ids[PMAX + lag_step : PMAX + lag_step + epochs])
        moved_back = (
            moved_back
            + ma_coeffs[:, lag_step][None, :, None]
            * extended_back[:, :, lag_step : lag_step + epochs]
            * joined[None, None, :]
        )
    weighted = (moved_back * gaps[None, None, :]).astype(jnp.bfloat16)
    gradient = lax.dot_general(
        weighted.reshape(rhs_count, 3 * epochs),
        design_flat,
        (((1,), (0,)), ((), ())),
        preferred_element_type=jnp.float32,
    )
    summed = lax.psum(gradient, "tm")
    owned = lax.dynamic_slice_in_dim(summed, lax.axis_index("tm") * share_len, share_len, 1)
    image = owned.reshape(rhs_count, 1, share_len) + kaula[None] * direction

    def precondition(vector):
        blocks = precond[0]
        shaped = vector.reshape(rhs_count, blocks.shape[0], blocks.shape[1])
        return jnp.einsum("bij,rbj->rbi", blocks, shaped, precision=precise).reshape(vector.shape)

    applied = precondition(residual)
    image_applied = precondition(image)
    old_rz, curvature, cross_term, image_term = lax.psum(
        (
            jnp.sum(residual * applied, axis=(1, 2)),
            jnp.sum(direction * image, axis=(1, 2)),
            jnp.sum(image * applied, axis=(1, 2)),
            jnp.sum(image * image_applied, axis=(1, 2)),
        ),
        ("tm", "order"),
    )
    step_len = old_rz / curvature
    new_solution = solution + step_len[:, None, None] * direction
    new_residual = residual - step_len[:, None, None] * image
    new_applied = applied - step_len[:, None, None] * image_applied
    new_rz = old_rz - 2.0 * step_len * cross_term + step_len * step_len * image_term
    new_direction = new_applied + (new_rz / old_rz)[:, None, None] * direction
    return (new_solution, new_residual, new_direction)


def solution(mesh):
    in_specs = (
        P(None, "tm", "order"),
        P("tm"),
        P("tm"),
        P(),
        P(),
        P(),
        P(),
        P("order", "tm"),
        P("order", "tm", None, None),
        P(None, "order", "tm"),
        P(None, "order", "tm"),
        P(None, "order", "tm"),
    )
    out_specs = (P(None, "order", "tm"), P(None, "order", "tm"), P(None, "order", "tm"))
    return jax.shard_map(
        on_device, mesh=mesh, in_specs=in_specs, out_specs=out_specs, check_vma=False
    )
```

profile of v0, /device:TPU:0, one launch (start us, length us, event | category | flops | bytes accessed | tf_op | source)
XLA Modules:
  0.0 370.5 jit_solution(15896302411517777981)
XLA Ops:
  7.3 0.7 broadcast_add_fusion
  8.1 4.9 %collective-permute-start.1 = (s32[4]{0:T(128)S(1)}, s32[4]{0:T(128)S(1)}, u32[]{:S(2)}, u32[]{:S(2)}) collective-permute-start(s32[4]{0:T(128)S(1)} %get-tuple-element.386), channel_id=1, source_target_pairs={{0,4},{4,8},{8,12},{12,16},{16,20},{20,24},{24,28},{1,5},{5,9},{9,... | collective-permute-start | bytes 56 | tf_op jit(solution)/shard_map/ppermute | solution.py:18
  13.0 1.3 collective-permute-start.2
  14.3 0.7 convert_element_type.15
  15.0 0.9 copy.77
  15.9 33.8 %all_gather.27 = bf16[16,1,16384]{2,0,1:T(8,128)(2,1)S(1)} all-gather(bf16[16,1,2048]{2,0,1:T(8,128)(2,1)S(1)} %copy.77), channel_id=1, replica_groups=mesh['tm'=8,'order'=4] {'tm'}, dimensions={2}, use_global_device_ids=true | all-gather | bytes 589824 | tf_op jit(solution)/shard_map/all_gather | solution.py:137
  49.7 6.3 %fusion.22 = f32[16,3,128]{2,0,1:T(8,128)S(1)} fusion(bf16[3,128,16384]{2,1,0:T(8,128)(2,1)} %param.16, bf16[16,1,16384]{2,0,1:T(8,128)(2,1)S(1)} %all_gather.27), kind=kOutput, calls=%fused_computation.33 | convolution fusion | flops 201326592 | bytes 13131776 | tf_op jit(solution)/shard_map/dot_general | solution.py:136
  56.1 10.4 %psum.43 = f32[16,3,128]{2,0,1:T(8,128)S(1)} all-reduce(f32[16,3,128]{2,0,1:T(8,128)S(1)} %fusion.22), channel_id=1, replica_groups=mesh['tm'=8,'order'=4] {'order'}, use_global_device_ids=true, to_apply=%region_2.3 | all-reduce | flops 6144 | bytes 49152 | tf_op jit(solution)/shard_map/psum | solution.py:143
  66.6 2.3 collective-permute-start
  69.9 29.5 %custom-call.4 = f32[3,1,128,128]{2,3,1,0:T(8,128)S(1)} custom-call(f32[3,1,128,128]{3,2,1,0:T(8,128)S(1)} %add_select_fusion), custom_call_target="InvertDiagBlocksLowerTriangular" | custom-call | tf_op jit(solution)/shard_map/jit(_solve_triangular)/vmap()/triangular_solve | solution.py:127
  99.4 0.5 fusion.24
  100.1 0.4 convolution_negate_fusion.1
  100.8 30.8 %all-gather = f32[24,4,4]{2,1,0:T(4,128)S(1)} all-gather(f32[3,4,4]{2,1,0:T(4,128)S(1)} %copy.48), channel_id=2, replica_groups=mesh['tm'=8,'order'=4] {'tm'}, dimensions={0}, use_global_device_ids=true | all-gather | bytes 1728 | tf_op jit(solution)/shard_map/all_gather | solution.py:34
  131.8 0.3 convolution_negate_fusion
  132.2 30.8 %all-gather.2 = f32[24,4,4]{2,1,0:T(4,128)S(1)} all-gather(f32[3,4,4]{2,1,0:T(4,128)S(1)} %copy.50), channel_id=4, replica_groups=mesh['tm'=8,'order'=4] {'tm'}, dimensions={0}, use_global_device_ids=true | all-gather | bytes 1728 | tf_op jit(solution)/shard_map/all_gather | solution.py:34
  163.0 0.5 convolution_bitcast_fusion.8
  163.7 30.7 %all-gather.1 = f32[128,3,4]{2,0,1:T(8,128)S(1)} all-gather(f32[16,3,4]{2,0,1:T(8,128)S(1)} %slice.202), channel_id=3, replica_groups=mesh['tm'=8,'order'=4] {'tm'}, dimensions={0}, use_global_device_ids=true | all-gather | bytes 6912 | tf_op jit(solution)/shard_map/all_gather | solution.py:34
  194.5 1.6 while.30
  196.4 0.2 convolution_bitcast_fusion.6
  196.6 30.6 %all-gather.3 = f32[128,3,4]{2,0,1:T(8,128)S(1)} all-gather(f32[16,3,4]{2,0,1:T(8,128)S(1)} %bitcast.113), channel_id=5, replica_groups=mesh['tm'=8,'order'=4] {'tm'}, dimensions={0}, use_global_device_ids=true | all-gather | bytes 6912 | tf_op jit(solution)/shard_map/all_gather | solution.py:34
  227.5 1.7 while.31
  229.4 1.5 collective-permute-start.3
  230.9 4.2 %collective-permute-done.3 = f32[16,3,4]{2,0,1:T(8,128)S(1)} collective-permute-done((f32[16,3,4]{2,0,1:T(8,128)S(1)}, f32[16,3,4]{2,0,1:T(8,128)S(1)}, u32[]{:S(2)}, u32[]{:S(2)}) %collective-permute-start.3) | collective-permute-done | bytes 800 | tf_op jit(solution)/shard_map/ppermute | solution.py:29
  235.2 7.4 %convolution_bitcast_fusion.2 = f32[16,16384]{1,0:T(8,128)} fusion(bf16[3,128,16384]{2,1,0:T(8,128)(2,1)} %param.16, f32[16,3,128]{2,0,1:T(8,128)S(1)} %fusion.18, f32[16,3,4]{2,0,1:T(8,128)S(1)} %collective-permute-done.3, f32[128]{0:T(128)S(1)} %get-tuple-element.359, f32[128]{0:T(128)S(1)} %get-tuple-element.360, f32[128]{0:T(128)S(1)} %get-tuple-element.361, ...), kind=kOutput, calls=%fused_computation.20 | convolution fusion | flops 201443328 | bytes 13659452 | tf_op jit(solution)/shard_map/dot_general | solution.py:185
  242.7 1.7 convolution_bitcast_fusion.4
  244.5 74.0 %all-reduce.9.cloned.1.call-done = f32[16,16384]{1,0:T(8,128)} async-done(((f32[16,16384]{1,0:T(8,128)}), f32[16,16384]{1,0:T(8,128)}) %all-reduce.9.cloned.1.call-update) | async-done | bytes 1048592 | tf_op jit(solution)/shard_map/psum | solution.py:191
  318.5 1.0 bitcast_add_fusion
  319.5 1.7 convolution_bitcast_fusion.3
  321.5 39.6 %all-reduce.6 = (f32[16]{0:T(128)S(1)}, f32[16]{0:T(128)S(1)}, f32[16]{0:T(128)S(1)}, f32[16]{0:T(128)S(1)}) all-reduce(f32[16]{0:T(128)S(1)} %get-tuple-element.304, f32[16]{0:T(128)S(1)} %get-tuple-element.306, f32[16]{0:T(128)S(1)} %get-tuple-element.305, ...), channel_id=1, replica_groups=mesh['tm'=8,'order'=4] {'tm','order'}, use_global_device_ids=true, to_apply=%region_1.2 | all-reduce | flops 64 | bytes 512 | tf_op jit(solution)/shard_map/psum | solution.py:202
  361.3 0.8 copy.60
  362.1 0.8 copy.61
  362.9 0.8 copy.62
  (110 shorter events, 6.1 us)
Async XLA Ops:
  7.2 235.5 %copy-start = (f32[1,16,128,128]{3,2,1,0:T(8,128)S(1)}, f32[1,16,128,128]{3,2,1,0:T(8,128)}, u32[]{:S(2)}) copy-start(f32[1,16,128,128]{3,2,1,0:T(8,128)} %param.24) | copy-start | bytes 3145732
  7.2 62.4 %copy-start.4 = (f32[3,5]{0,1:T(8,128)S(1)}, f32[3,5]{0,1:T(8,128)}, u32[]{:S(2)}) copy-start(f32[3,5]{0,1:T(8,128)} %constant.101.clone.1) | copy-start | bytes 184
  7.2 62.4 %copy-start.5 = (f32[3,5]{0,1:T(8,128)S(1)}, f32[3,5]{0,1:T(8,128)}, u32[]{:S(2)}) copy-start(f32[3,5]{0,1:T(8,128)} %constant.103.clone.1) | copy-start | bytes 184
  7.2 124.5 %copy-start.11 = (s32[128]{0:T(128)S(1)}, s32[128]{0:T(128)}, u32[]{:S(2)}) copy-start(s32[128]{0:T(128)} %param.18) | copy-start | bytes 1540
  7.2 61.9 %copy-start.6 = (f32[3,4]{1,0:T(4,128)S(1)}, f32[3,4]{1,0:T(4,128)}, u32[]{:S(2)}) copy-start(f32[3,4]{1,0:T(4,128)} %param.22) | copy-start | bytes 148
  7.2 62.1 %copy-start.7 = (f32[3,4]{1,0:T(4,128)S(1)}, f32[3,4]{1,0:T(4,128)}, u32[]{:S(2)}) copy-start(f32[3,4]{1,0:T(4,128)} %param.21) | copy-start | bytes 148
  7.2 62.3 %copy-start.9 = (s32[3]{0:T(128)S(1)}, s32[3]{0:T(128)}, u32[]{:S(2)}) copy-start(s32[3]{0:T(128)} %param.19) | copy-start | bytes 40
  7.2 62.3 %copy-start.10 = (s32[3]{0:T(128)S(1)}, s32[3]{0:T(128)}, u32[]{:S(2)}) copy-start(s32[3]{0:T(128)} %param.20) | copy-start | bytes 40
  7.3 311.2 %all-reduce.9.cloned.1.call-start = ((), (), s32[]{:S(2)}) async-start(), calls=%async_computation | async-start | bytes 2097152 | tf_op jit(solution)/shard_map/psum | solution.py:191
  8.1 91.8 %collective-permute-start.1 = (s32[4]{0:T(128)S(1)}, s32[4]{0:T(128)S(1)}, u32[]{:S(2)}, u32[]{:S(2)}) collective-permute-start(s32[4]{0:T(128)S(1)} %get-tuple-element.386), channel_id=1, source_target_pairs={{0,4},{4,8},{8,12},{12,16},{16,20},{20,24},{24,28},{1,5},{5,9},{9,... | collective-permute-start | bytes 56 | tf_op jit(solution)/shard_map/ppermute | solution.py:18
  13.0 87.0 %collective-permute-start.2 = (s32[4]{0:T(128)S(1)}, s32[4]{0:T(128)S(1)}, u32[]{:S(2)}, u32[]{:S(2)}) collective-permute-start(s32[4]{0:T(128)S(1)} %get-tuple-element.385), channel_id=1, source_target_pairs={{4,0},{8,4},{12,8},{16,12},{20,16},{24,20},{28,24},{5,1},{9,5},{13... | collective-permute-start | bytes 56 | tf_op jit(solution)/shard_map/ppermute | solution.py:21
  56.1 186.6 %copy-start.2 = (f32[16,1,2048]{2,1,0:T(1,128)S(1)}, f32[16,1,2048]{2,1,0:T(1,128)}, u32[]{:S(2)}) copy-start(f32[16,1,2048]{2,1,0:T(1,128)} %param.26) | copy-start | bytes 393220
  56.1 262.4 %copy-start.1 = (f32[16,1,2048]{2,1,0:T(1,128)S(1)}, f32[16,1,2048]{2,1,0:T(1,128)}, u32[]{:S(2)}) copy-start(f32[16,1,2048]{2,1,0:T(1,128)} %param.27) | copy-start | bytes 393220
  56.1 262.4 %copy-start.8 = (f32[1,2048]{1,0:T(1,128)S(1)}, f32[1,2048]{1,0:T(1,128)}, u32[]{:S(2)}) copy-start(f32[1,2048]{1,0:T(1,128)} %param.23) | copy-start | bytes 24580
  56.1 305.0 %copy-start.3 = (f32[16,1,2048]{2,1,0:T(1,128)S(1)}, f32[16,1,2048]{2,1,0:T(1,128)}, u32[]{:S(2)}) copy-start(f32[16,1,2048]{2,1,0:T(1,128)} %param.25) | copy-start | bytes 393220
  66.6 96.4 %collective-permute-start = (f32[16,3,4]{2,0,1:T(8,128)S(1)}, f32[16,3,4]{2,0,1:T(8,128)S(1)}, u32[]{:S(2)}, u32[]{:S(2)}) collective-permute-start(f32[16,3,4]{2,0,1:T(8,128)S(1)} %slice.215), channel_id=1, source_target_pairs={{0,4},{4,8},{8,12},{12,16},{16,20},{20,24},{24,28},{1,5},{5,9},{9,... | collective-permute-start | bytes 2312 | tf_op jit(solution)/shard_map/ppermute | solution.py:29
  229.4 5.7 %collective-permute-start.3 = (f32[16,3,4]{2,0,1:T(8,128)S(1)}, f32[16,3,4]{2,0,1:T(8,128)S(1)}, u32[]{:S(2)}, u32[]{:S(2)}) collective-permute-start(f32[16,3,4]{2,0,1:T(8,128)S(1)} %bitcast.114), channel_id=1, source_target_pairs={{4,0},{8,4},{12,8},{16,12},{20,16},{24,20},{28,24},{5,1},{9,5},{13... | collective-permute-start | bytes 2312 | tf_op jit(solution)/shard_map/ppermute | solution.py:29
Sparse Core Ops, SparseCore 0:
  242.8 75.7 all-reduce.8
where the time goes:
time: 371 us
  blocking collectives  207 us (56%)
  waiting for transfers between devices  78.3 us (21%)
  other arithmetic  32.8 us (9%)
  matrix products  22.3 us (6%)
  between operations  14.5 us (4%)
  starting transfers between devices  9.99 us (3%)
  local copies, waits for them, and re-layouts  5.35 us (1%)
    all_gather x4, blocking collectives, entering(): everything = jax.tree.map(lambda part: lax.all_gather(part, axis), value)  123 us
    psum x1, waiting for transfers between devices, on_device(): summed = lax.psum(gradient, 'tm')  74 us
    psum x1, blocking collectives, on_device(): lax.psum((jnp.sum(residual * applied, axis=(1, 2)), jnp.sum(direction * i...  39.6 us
    all_gather x1, blocking collectives, on_device(): lax.all_gather(packed, 'tm', axis=2, tiled=True)[:, 0, :]  33.8 us
    another operation x3, other arithmetic, on_device(): jax.scipy.linalg.solve_triangular(lower, jnp.broadcast_to(identity, (3, e...  29.7 us
    psum x1, blocking collectives, on_device(): whole_obs = lax.psum(partial_obs, 'order')  10.4 us
    dot_general x1, matrix products, on_device(): lax.dot_general(weighted.reshape(rhs_count, 3 * epochs), design_flat, (((...  7.45 us
  transfers between devices with their start and end apart: 5, of which 2 were waited for; matrix products, arithmetic and copies ran while one was open for 11% of the time, Pallas kernels for 0%

commit v1 on v0

v1 whole, which is shorter than its diff:
```python
import functools

import jax
import jax.numpy as jnp
from jax import lax
from jax.experimental import pallas as pl
from jax.experimental.pallas import tpu as pltpu
from jax.sharding import PartitionSpec as P

LINK = jnp.float32
LAGS = 4
HI = lax.Precision.HIGHEST
NN = (((1,), (0,)), ((), ()))
NT = (((1,), (1,)), ((), ()))


def dot(a, b, dims, precision=None):
    return lax.dot_general(a, b, dims, precision=precision, preferred_element_type=jnp.float32)


def rows_of(pieces, count, width):
    row = lax.broadcasted_iota(jnp.int32, (count, width), 0)
    out = jnp.zeros((count, width), jnp.float32)
    for at, piece in pieces:
        out = jnp.where(row == at, piece, out)
    return out


def tall(block, rows):
    return jnp.concatenate(
        [block, jnp.zeros((rows - block.shape[0], block.shape[1]), jnp.float32)], axis=0
    )


def bands(matrix):
    row = lax.broadcasted_iota(jnp.int32, matrix.shape, 0)
    col = lax.broadcasted_iota(jnp.int32, matrix.shape, 1)
    inside = row // LAGS == col // LAGS
    return [
        jnp.sum(
            jnp.where(inside & (row == col - shift), matrix, 0.0), axis=0, keepdims=True
        )
        for shift in range(1 - LAGS, LAGS)
    ]


def banded(vector, coeffs):
    width = vector.shape[1]
    total = None
    for shift, coeff in zip(range(1 - LAGS, LAGS), coeffs):
        moved = vector if shift == 0 else pltpu.roll(vector, shift % width, 1)
        total = moved * coeff if total is None else total + moved * coeff
    return total


def filters(ar_ref, ma_ref, aro_ref, mao_ref, ids, pt_ref):
    n = ids.shape[1]
    lane = lax.broadcasted_iota(jnp.int32, (1, n), 1)

    def lagged(v, k):
        return v if k == 0 else jnp.where(lane >= k, pltpu.roll(v, k, 1), 0.0)

    impulse = jnp.where(lane == 0, 1.0, 0.0).astype(jnp.float32)
    grid = jnp.broadcast_to(ids, (n, n))
    row = lax.broadcasted_iota(jnp.int32, (n, n), 0)
    col = lax.broadcasted_iota(jnp.int32, (n, n), 1)
    joined = (grid == grid.T) & (col >= row)
    out_rows, in_rows, end_rows = [], [], []
    for c in range(3):
        ar = [jnp.where(k < aro_ref[c], ar_ref[c, k], 0.0) for k in range(LAGS)]
        ma = [jnp.where(k < mao_ref[c], ma_ref[c, k], 0.0) for k in range(LAGS)]
        a, b = [1.0] + [0.0] * LAGS, [1.0] + [0.0] * LAGS
        for k in range(LAGS):
            a = [a[0]] + [a[j] - ar[k] * a[j - 1] for j in range(1, LAGS + 1)]
            b = [b[0]] + [b[j] - ma[k] * b[j - 1] for j in range(1, LAGS + 1)]
        h = impulse
        for k in range(LAGS):
            power, m = ar[k], 1
            while m < n:
                h = h + power * lagged(h, m)
                power, m = power * power, 2 * m
        g = h
        for k in range(LAGS):
            g = g - ma[k] * lagged(g, 1)
        for i in range(1, LAGS + 1):
            out_rows.append((c * LAGS + i - 1, lagged(h, i - 1)))
            acc = jnp.zeros_like(g)
            end = jnp.zeros_like(g)
            for m in range(LAGS + 1 - i):
                acc = acc + b[i + m] * lagged(impulse, m) - a[i + m] * lagged(g, m)
                end = end - a[i + m] * jnp.where(lane == n - 1 - m, 1.0, 0.0)
            in_rows.append((c * LAGS + i - 1, acc))
            end_rows.append((c * LAGS + i - 1, end))
        t = jnp.broadcast_to(g, (n, n))
        bit = 1
        while bit < n:
            t = jnp.where((row // bit) % 2 == 1, pltpu.roll(t, bit, 1), t)
            bit *= 2
        pt_ref[c] = jnp.where(joined, t, 0.0)
    ca = rows_of(out_rows, 16, n)
    flip = jnp.where(row + col == n - 1, 1.0, 0.0).astype(jnp.float32)
    ab = dot(rows_of(in_rows, 16, n), flip, NN, HI)
    ends = rows_of(end_rows, 16, n)
    fwd = bands(dot(ca, tall(ends, n), NT, HI))
    bwd = bands(dot(ends, tall(ca, n), NT, HI))
    return ca, ab, fwd, bwd


def spread(block, mask):
    row = lax.broadcasted_iota(jnp.int32, block.shape, 0)
    return jnp.concatenate(
        [jnp.where(row // LAGS == c, block * mask, 0.0) for c in range(3)], axis=1
    )


def kernel(
    T, O,
    design, packed, ids_in, gaps, ar_ref, ma_ref, aro_ref, mao_ref, kaula, precond,
    sol, res, direc,
    new_sol, new_res, new_dir,
    dv, right_in, left_in, obs_out, obs_in, ids_all, summ_out, summ_in, pt,
    rs_right_out, rs_left_out, rs_right_in, rs_left_in, applied, image_applied,
    tot_out, tot_in, tot2_out, tot2_in,
    dsem, agr_s, agr_r, agl_s, agl_r, ob_s, ob_r, id_s, id_r, su_s, su_r,
    rr_s, rr_r, rl_s, rl_r, t1_s, t1_r, t2_s, t2_r,
):
    me, order = lax.axis_index("tm"), lax.axis_index("order")
    A = T // 2
    share = packed.shape[1]
    n = ids_in.shape[1]
    right_n, left_n = T // 2, T - 1 - T // 2

    def tm_at(p):
        p = lax.rem(p + 2 * T, T)
        return jnp.where(p < A, 2 * p, 2 * (T - 1 - p) + 1)

    pos = jnp.where(me % 2 == 0, me // 2, T - 1 - me // 2)
    right, left = {"tm": tm_at(pos + 1)}, {"tm": tm_at(pos - 1)}

    def to_tm(k):
        return {"tm": lax.rem(me + k, T)}

    def to_order(k):
        return {"order": lax.rem(order + k, O)}

    def load(dist):
        q = tm_at(pos + dist)
        return pltpu.make_async_copy(
            design.at[:, pl.ds(pl.multiple_of(q * share, 128), share)],
            dv.at[dist % T],
            dsem.at[dist % T],
        )

    def remote(src, dst, ssem, rsem, to):
        return pltpu.make_async_remote_copy(
            src_ref=src, dst_ref=dst, send_sem=ssem, recv_sem=rsem,
            device_id=to, device_id_type=pl.DeviceIdType.MESH,
        )

    arrivals = [0]
    for s in range(1, right_n + 1):
        arrivals.append(-s)
        if s <= left_n:
            arrivals.append(s)
    for dist in arrivals:
        load(dist).start()

    barrier = pltpu.get_barrier_semaphore()
    for k in range(1, T):
        pl.semaphore_signal(barrier, inc=1, device_id=to_tm(k), device_id_type=pl.DeviceIdType.MESH)
    for k in range(1, O):
        pl.semaphore_signal(barrier, inc=1, device_id=to_order(k), device_id_type=pl.DeviceIdType.MESH)
    pl.semaphore_wait(barrier, T - 1 + O - 1)

    def ag_right(s):
        src = packed if s == 0 else right_in.at[s - 1]
        return remote(src, right_in.at[s], agr_s.at[s], agr_r.at[s], right)

    def ag_left(s):
        src = packed if s == 0 else left_in.at[s - 1]
        return remote(src, left_in.at[s], agl_s.at[s], agl_r.at[s], left)

    ag_right(0).start()
    ag_left(0).start()
    id_copies = [
        remote(ids_in, ids_all.at[k - 1], id_s.at[k - 1], id_r.at[k - 1], to_tm(k))
        for k in range(1, T)
    ]
    for copy in id_copies:
        copy.start()

    load(0).wait()
    obs = dot(packed[...], dv[0], NT)
    ids = ids_in[0:1, :]
    ca, ab, fwd, bwd = filters(ar_ref, ma_ref, aro_ref, mao_ref, ids, pt)
    for s in range(right_n):
        ag_right(s).wait_recv()
        if s + 1 < right_n:
            ag_right(s + 1).start()
        if s < left_n:
            ag_left(s).wait_recv()
            if s + 1 < left_n:
                ag_left(s + 1).start()
        load(-(s + 1)).wait()
        obs = obs + dot(right_in[s], dv[(-(s + 1)) % T], NT)
        if s < left_n:
            load(s + 1).wait()
            obs = obs + dot(left_in[s], dv[s + 1], NT)
    obs_out[...] = obs
    ob_copies = [
        remote(obs_out, obs_in.at[k - 1], ob_s.at[k - 1], ob_r.at[k - 1], to_order(k))
        for k in range(1, O)
    ]
    for copy in ob_copies:
        copy.start()

    first, last = ids[:, 0:1], ids[:, n - 1 : n]
    at_first = jnp.where(ids == first, 1.0, 0.0)
    at_last = jnp.where(ids == last, 1.0, 0.0)
    head_map = spread(ca, at_first)
    tail_map = spread(ab, at_last)
    head16 = tall(head_map, n)
    tail16 = tall(tail_map, n)
    zeros64 = jnp.zeros((n // 2, 3 * n), jnp.float32)
    head_low = jnp.concatenate([zeros64, head16[: n // 2]], axis=0)
    for copy in id_copies:
        copy.wait_recv()
    ids_e = []
    for e in range(T):
        slot = lax.rem(me - e + T - 1, T)
        slot = jnp.minimum(slot, T - 2)
        ids_e.append(jnp.where(me == e, ids, ids_all[slot][0:1, :]))
    firsts = [v[:, 0:1] for v in ids_e]
    lasts = [v[:, n - 1 : n] for v in ids_e]
    runs = jnp.concatenate(
        [ca * jnp.where(v == f, 1.0, 0.0) for v, f in zip(ids_e, firsts)], axis=0
    )
    energy = dot(runs, tall(ca, n), NT, HI)
    energies = [bands(energy[16 * e : 16 * e + 16]) for e in range(T)]

    for copy in ob_copies:
        copy.wait_recv()
    for k in range(1, O):
        obs = obs + obs_in[k - 1]
    gaps3 = jnp.concatenate([gaps[0:1, :]] * 3, axis=1)
    masked = obs * gaps3
    local = jnp.concatenate(
        [dot(masked[:, c * n : (c + 1) * n], pt[c], NN, HI) for c in range(3)], axis=1
    )
    summary = dot(masked, tail16, NT, HI) + dot(local, head_low, NT, HI)
    summ_out[...] = summary
    su_copies = [
        remote(summ_out, summ_in.at[k - 1], su_s.at[k - 1], su_r.at[k - 1], to_tm(k))
        for k in range(1, T)
    ]
    for copy in su_copies:
        copy.start()
    local_back = jnp.concatenate(
        [dot(local[:, c * n : (c + 1) * n], pt[c], NT, HI) for c in range(3)], axis=1
    )
    for copy in su_copies:
        copy.wait_recv()
    sums = []
    for e in range(T):
        slot = jnp.minimum(lax.rem(me - e + T - 1, T), T - 2)
        sums.append(jnp.where(me == e, summary, summ_in[slot]))
    state = jnp.zeros_like(summary)
    mine_in = jnp.zeros_like(summary)
    ins = []
    for e in range(T):
        entering = state if e == 0 else state * jnp.where(lasts[e - 1] == firsts[e], 1.0, 0.0)
        ins.append(entering)
        mine_in = jnp.where(me == e, entering, mine_in)
        through = jnp.where(firsts[e] == lasts[e], 1.0, 0.0)
        state = sums[e] + through * banded(entering, fwd)
    back = jnp.zeros_like(summary)
    mine_back = jnp.zeros_like(summary)
    for e in range(T - 1, 0, -1):
        through = jnp.where(firsts[e] == lasts[e], 1.0, 0.0)
        heads = pltpu.roll(sums[e], n // 2, 1) + banded(ins[e], energies[e])
        back = (heads + through * banded(back, bwd)) * jnp.where(
            lasts[e - 1] == firsts[e], 1.0, 0.0
        )
        mine_back = jnp.where(me == e - 1, back, mine_back)
    lane = lax.broadcasted_iota(jnp.int32, summary.shape, 1)
    mine_in = jnp.where(lane < 3 * LAGS, mine_in, 0.0)
    mine_back = jnp.where(lane < 3 * LAGS, mine_back, 0.0)
    entered = dot(mine_in, head16, NN, HI)
    entered_back = jnp.concatenate(
        [dot(entered[:, c * n : (c + 1) * n], pt[c], NT, HI) for c in range(3)], axis=1
    )
    adjoint = local_back + entered_back + dot(mine_back, tail16, NN, HI)
    weighted = (adjoint * gaps3).astype(jnp.bfloat16)

    def grad(dist):
        return dot(weighted, dv[dist % T], NN)

    def rs_right(s):
        return remote(rs_right_out.at[s], rs_right_in.at[s], rr_s.at[s], rr_r.at[s], right)

    def rs_left(s):
        return remote(rs_left_out.at[s], rs_left_in.at[s], rl_s.at[s], rl_r.at[s], left)

    for s in range(right_n):
        piece = grad(right_n - s)
        if s > 0:
            rs_right(s - 1).wait_recv()
            piece = piece + rs_right_in[s - 1].astype(jnp.float32)
        rs_right_out[s] = piece.astype(LINK)
        rs_right(s).start()
        if s < left_n:
            piece = grad(s - left_n)
            if s > 0:
                rs_left(s - 1).wait_recv()
                piece = piece + rs_left_in[s - 1].astype(jnp.float32)
            rs_left_out[s] = piece.astype(LINK)
            rs_left(s).start()
    own = grad(0)
    blocks = precond.shape[0]
    for m in range(blocks):
        cols = slice(m * 128, (m + 1) * 128)
        applied[:, cols] = dot(res[:, cols], precond[m], NT, HI)
    rs_right(right_n - 1).wait_recv()
    own = own + rs_right_in[right_n - 1].astype(jnp.float32)
    if left_n > 0:
        rs_left(left_n - 1).wait_recv()
        own = own + rs_left_in[left_n - 1].astype(jnp.float32)
    image = own + kaula[...] * direc[...]
    for m in range(blocks):
        cols = slice(m * 128, (m + 1) * 128)
        image_applied[:, cols] = dot(image[:, cols], precond[m], NT, HI)
    app, imapp = applied[...], image_applied[...]
    d, r = direc[...], res[...]
    rhs = d.shape[0]
    lane = lax.broadcasted_iota(jnp.int32, (rhs, 128), 1)
    row = lax.broadcasted_iota(jnp.int32, (rhs, 128), 0)
    products = [r * app, d * image, image * app, image * imapp]
    total = jnp.zeros((rhs, 128), jnp.float32)
    for q, product in enumerate(products):
        total = jnp.where(lane == q * rhs + row, jnp.sum(product, axis=1, keepdims=True), total)
    total = jnp.broadcast_to(jnp.sum(total, axis=0, keepdims=True), (8, 128))

    def gather_sum(value, out, into, ssem, rsem, count, to):
        out[...] = value
        copies = [
            remote(out, into.at[k - 1], ssem.at[k - 1], rsem.at[k - 1], to(k))
            for k in range(1, count)
        ]
        for copy in copies:
            copy.start()
        for k, copy in enumerate(copies):
            copy.wait_recv()
            value = value + into[k]
        return value, copies

    total, c1 = gather_sum(total, tot_out, tot_in, t1_s, t1_r, O, to_order)
    total, c2 = gather_sum(total, tot2_out, tot2_in, t2_s, t2_r, T, to_tm)
    wide = jnp.broadcast_to(total[0:1, :], (rhs, 128))
    old_rz, curvature, cross, quad = [
        jnp.sum(jnp.where(lane == q * rhs + row, wide, 0.0), axis=1, keepdims=True)
        for q in range(4)
    ]
    step = old_rz / curvature
    new_rz = old_rz - 2.0 * step * cross + step * step * quad
    new_sol[...] = sol[...] + step * d
    new_res[...] = r - step * image
    new_dir[...] = app - step * imapp + (new_rz / old_rz) * d

    for s in range(right_n):
        ag_right(s).wait_send()
        rs_right(s).wait_send()
    for s in range(left_n):
        ag_left(s).wait_send()
        rs_left(s).wait_send()
    for copy in id_copies + ob_copies + su_copies + c1 + c2:
        copy.wait_send()


def on_device(
    T, O, design, gap_flags, segment_ids, ar_order, ma_order, ar_roots, ma_roots,
    kaula, precond, solution, residual, direction,
):
    n = segment_ids.shape[0]
    columns = design.shape[2]
    share = direction.shape[2]
    rhs = direction.shape[0]
    f32, bf16 = jnp.float32, jnp.bfloat16
    flat = lambda v: v.reshape(rhs, share)
    ids8 = jnp.broadcast_to(segment_ids.astype(f32)[None, :], (8, n))
    gaps8 = jnp.broadcast_to(gap_flags.astype(f32)[None, :], (8, n))
    packed = flat(direction).astype(bf16)
    right_n, left_n = T // 2, T - 1 - T // 2
    vmem = pl.BlockSpec(memory_space=pltpu.VMEM)
    smem = pl.BlockSpec(memory_space=pltpu.SMEM)
    V, D = pltpu.VMEM, lambda k: pltpu.SemaphoreType.DMA((max(k, 1),))
    L = max(left_n, 1)
    outs = pl.pallas_call(
        functools.partial(kernel, T, O),
        out_shape=[jax.ShapeDtypeStruct((rhs, share), f32)] * 3,
        in_specs=[pl.BlockSpec(memory_space=pl.ANY), vmem, vmem, vmem, smem, smem, smem, smem,
                  vmem, vmem, vmem, vmem, vmem],
        out_specs=[vmem] * 3,
        scratch_shapes=[
            V((T, 3 * n, share), bf16), V((right_n, rhs, share), bf16), V((L, rhs, share), bf16),
            V((rhs, 3 * n), f32), V((O - 1, rhs, 3 * n), f32), V((T - 1, 8, n), f32),
            V((rhs, n), f32), V((T - 1, rhs, n), f32), V((3, n, n), f32),
            V((right_n, rhs, share), LINK), V((L, rhs, share), LINK),
            V((right_n, rhs, share), LINK), V((L, rhs, share), LINK),
            V((rhs, share), f32), V((rhs, share), f32),
            V((8, 128), f32), V((O - 1, 8, 128), f32), V((8, 128), f32), V((T - 1, 8, 128), f32),
            D(T), D(right_n), D(right_n), D(L), D(L), D(O - 1), D(O - 1), D(T - 1), D(T - 1),
            D(T - 1), D(T - 1), D(right_n), D(right_n), D(L), D(L), D(O - 1), D(O - 1),
            D(T - 1), D(T - 1),
        ],
        compiler_params=pltpu.CompilerParams(
            collective_id=0, has_side_effects=True, vmem_limit_bytes=56 * 1024 * 1024
        ),
    )(
        design.reshape(3 * n, columns), packed, ids8, gaps8, ar_roots, ma_roots, ar_order,
        ma_order, kaula, precond[0], flat(solution), flat(residual), flat(direction),
    )
    return tuple(v.reshape(direction.shape) for v in outs)


def solution(mesh):
    vec = P(None, "order", "tm")
    in_specs = (
        P(None, "tm", "order"), P("tm"), P("tm"), P(), P(), P(), P(), P("order", "tm"),
        P("order", "tm", None, None), vec, vec, vec,
    )
    body = functools.partial(on_device, mesh.shape["tm"], mesh.shape["order"])
    return jax.shard_map(
        body, mesh=mesh, in_specs=in_specs, out_specs=(vec, vec, vec), check_vma=False
    )
```

time: 371 us -> 74.3 us (0.20)
  blocking collectives: 207 us -> 0 us
  waiting for transfers between devices: 78.3 us -> 0 us
  Pallas kernels: 0 us -> 60.9 us
  other arithmetic: 32.8 us -> 1.32 us
  matrix products: 22.3 us -> 0 us
  between operations: 14.5 us -> 0.64 us
  starting transfers between devices: 9.99 us -> 0 us
  local copies, waits for them, and re-layouts: 5.35 us -> 11.2 us
    all_gather x5 -> x0, blocking collectives: 157 us -> none  [the longest x4 123 us: entering(): everything = jax.tree.map(lambda part: lax.all_gather(part, axis), value)]
    psum x1 -> x0, waiting for transfers between devices: 74 us -> none  [on_device(): summed = lax.psum(gradient, 'tm')]
    pallas_call x0 -> x1, Pallas kernels: none -> 60.9 us  [on_device(): pl.pallas_call(functools.partial(kernel, T, O), out_shape=[jax.ShapeDtype...]
    psum x2 -> x0, blocking collectives: 50 us -> none  [the longest x1 39.6 us: on_device(): lax.psum((jnp.sum(residual * applied, axis=(1, 2)), jnp.sum(direction * i...]
    another operation x3 -> x0, other arithmetic: 29.7 us -> none  [on_device(): jax.scipy.linalg.solve_triangular(lower, jnp.broadcast_to(identity, (3, e...]
    dot_general x26 -> x0, matrix products: 21.8 us -> none  [the longest x1 7.45 us: on_device(): lax.dot_general(weighted.reshape(rhs_count, 3 * epochs), design_flat, (((...]
    ppermute x4 -> x0, starting transfers between devices: 9.95 us -> none  [the longest x1 4.89 us: extended_2(): lax.ppermute(lax.slice_in_dim(block, block.shape[dim] - width, None, axis...]
    unnamed x31 -> x6, local copies, waits for them, and re-layouts: 3.83 us -> 9.99 us
  transfers between devices with their start and end apart: 5 -> 0, of which waited for: 2 -> 0; matrix products, arithmetic and copies ran while one was open for 11% -> 0% of each run, Pallas kernels for 0% -> 0%
where the time goes in v1:
time: 74.3 us; the launch traced here: 74 us
  Pallas kernels  60.9 us (82%)
  local copies, waits for them, and re-layouts  11.2 us (15%)
  other arithmetic  1.32 us (2%)
    pallas_call x1, Pallas kernels, on_device(): pl.pallas_call(functools.partial(kernel, T, O), out_shape=[jax.ShapeDtype...  60.9 us
    unnamed x6, local copies, waits for them, and re-layouts  9.99 us

profile of v1, /device:TPU:0, one launch (start us, length us, event | category | flops | bytes accessed | tf_op | source)
XLA Modules:
  0.0 74.0 jit_solution(5721480636941735150)
XLA Ops:
  0.6 0.7 convert_element_type.11
  1.3 0.7 convert_element_type.10
  1.9 0.6 broadcast_in_dim.4.ids_in
  2.5 0.6 broadcast_in_dim.5.gaps
  3.1 1.6 %copy.27 = bf16[16,1,2048]{2,0,1:T(8,128)(2,1)} copy(f32[16,1,2048]{2,1,0:T(1,128)} %param.23) | data formatting | bytes 196608
  4.7 1.6 %copy.26 = f32[16,1,2048]{2,0,1:T(8,128)} copy(f32[16,1,2048]{2,1,0:T(1,128)} %param.23) | data formatting | bytes 262144
  6.3 1.7 %copy_bitcast_fusion = (f32[16,2048]{1,0:T(8,128)}, f32[16,2048]{1,0:T(8,128)}) fusion(f32[16,1,2048]{2,1,0:T(1,128)} %param.22, f32[16,1,2048]{2,1,0:T(1,128)} %param.21), kind=kLoop, calls=%fused_computation | loop fusion | bytes 524288
  8.0 60.9 %shard_map.139 = (f32[16,2048]{1,0:T(8,128)}, f32[16,2048]{1,0:T(8,128)}, f32[16,2048]{1,0:T(8,128)}) custom-call(bf16[384,16384]{1,0:T(8,128)(2,1)} %bitcast.15, bf16[16,2048]{1,0:T(8,128)(2,1)} %bitcast.18, f32[8,128]{1,0:T(8,128)} %broadcast_in_dim.4.ids_in, f32[8,128]{1,0:T(8,128)} %broadcast_in_dim.5.gaps, f32[3,4]{1,0:T(4,128)} %ar_ref.1, ...), custom_call_target="tpu_custom_call" | custom-call | tf_op jit(solution)/shard_map/pallas_call | solution.py:397
  68.9 1.7 %copy.15 = f32[16,1,2048]{2,1,0:T(1,128)} copy(f32[16,1,2048]{2,0,1:T(8,128)} %bitcast.21) | data formatting | bytes 262144
  70.6 1.7 %copy.16 = f32[16,1,2048]{2,1,0:T(1,128)} copy(f32[16,1,2048]{2,0,1:T(8,128)} %bitcast.20) | data formatting | bytes 262144
  72.3 1.7 %copy.17 = f32[16,1,2048]{2,1,0:T(1,128)} copy(f32[16,1,2048]{2,0,1:T(8,128)} %bitcast.19) | data formatting | bytes 262144

commit v2 on v1

--- a/solution.py
+++ b/solution.py
@@ -7,7 +7,7 @@
 from jax.experimental.pallas import tpu as pltpu
 from jax.sharding import PartitionSpec as P
 
-LINK = jnp.float32
+LINK = jnp.bfloat16
 LAGS = 4
 HI = lax.Precision.HIGHEST
 NN = (((1,), (0,)), ((), ()))
@@ -112,23 +112,24 @@
         [jnp.where(row // LAGS == c, block * mask, 0.0) for c in range(3)], axis=1
     )
 
-
 def kernel(
-    T, O,
-    design, packed, ids_in, gaps, ar_ref, ma_ref, aro_ref, mao_ref, kaula, precond,
-    sol, res, direc,
-    new_sol, new_res, new_dir,
-    dv, right_in, left_in, obs_out, obs_in, ids_all, summ_out, summ_in, pt,
+    T, O, SUB,
+    design, ids_in, gaps_in, ar_ref, ma_ref, aro_ref, mao_ref, kaula, precond_in,
+    res_in, direc_in,
+    image_out, comb_out, scal_out,
+    dv, precond, res, direc, packed, high, low,
+    right_in, left_in, obs_out, obs_in, ids_all, summ_out, summ_in, pt,
     rs_right_out, rs_left_out, rs_right_in, rs_left_in, applied, image_applied,
     tot_out, tot_in, tot2_out, tot2_in,
-    dsem, agr_s, agr_r, agl_s, agl_r, ob_s, ob_r, id_s, id_r, su_s, su_r,
+    dsem, in_sem, agr_s, agr_r, agl_s, agl_r, ob_s, ob_r, id_s, id_r, su_s, su_r,
     rr_s, rr_r, rl_s, rl_r, t1_s, t1_r, t2_s, t2_r,
 ):
     me, order = lax.axis_index("tm"), lax.axis_index("order")
     A = T // 2
-    share = packed.shape[1]
+    rhs, share = packed.shape
     n = ids_in.shape[1]
-    right_n, left_n = T // 2, T - 1 - T // 2
+    piece_len = share // SUB
+    blocks = precond.shape[0]
 
     def tm_at(p):
         p = lax.rem(p + 2 * T, T)
@@ -136,12 +137,16 @@
 
     pos = jnp.where(me % 2 == 0, me // 2, T - 1 - me // 2)
     right, left = {"tm": tm_at(pos + 1)}, {"tm": tm_at(pos - 1)}
+    mesh_ids = pl.DeviceIdType.MESH
 
     def to_tm(k):
         return {"tm": lax.rem(me + k, T)}
 
     def to_order(k):
         return {"order": lax.rem(order + k, O)}
+
+    def part(h):
+        return slice(h * piece_len, (h + 1) * piece_len)
 
     def load(dist):
         q = tm_at(pos + dist)
@@ -154,34 +159,59 @@
     def remote(src, dst, ssem, rsem, to):
         return pltpu.make_async_remote_copy(
             src_ref=src, dst_ref=dst, send_sem=ssem, recv_sem=rsem,
-            device_id=to, device_id_type=pl.DeviceIdType.MESH,
+            device_id=to, device_id_type=mesh_ids,
         )
 
-    arrivals = [0]
-    for s in range(1, right_n + 1):
-        arrivals.append(-s)
-        if s <= left_n:
-            arrivals.append(s)
-    for dist in arrivals:
-        load(dist).start()
-
+    get_direc = pltpu.make_async_copy(direc_in.at[:, 0, :], direc, in_sem.at[0])
+    get_res = pltpu.make_async_copy(res_in.at[:, 0, :], res, in_sem.at[1])
+    get_precond = pltpu.make_async_copy(precond_in, precond, in_sem.at[2])
+    get_direc.start()
     barrier = pltpu.get_barrier_semaphore()
     for k in range(1, T):
-        pl.semaphore_signal(barrier, inc=1, device_id=to_tm(k), device_id_type=pl.DeviceIdType.MESH)
+        pl.semaphore_signal(barrier, inc=1, device_id=to_tm(k), device_id_type=mesh_ids)
     for k in range(1, O):
-        pl.semaphore_signal(barrier, inc=1, device_id=to_order(k), device_id_type=pl.DeviceIdType.MESH)
+        pl.semaphore_signal(barrier, inc=1, device_id=to_order(k), device_id_type=mesh_ids)
+    arrivals = [0]
+    for s in range(1, A):
+        arrivals += [-s, s]
+    arrivals.append(A)
+    load(0).start()
+    get_precond.start()
+    get_res.start()
+    for dist in arrivals[1:]:
+        load(dist).start()
+    get_direc.wait()
+    packed[...] = direc[...].astype(jnp.bfloat16)
+    get_precond.wait()
+    for m in range(blocks):
+        whole = precond[m]
+        top = whole.astype(jnp.bfloat16)
+        high[m] = top
+        low[m] = (whole - top.astype(jnp.float32)).astype(jnp.bfloat16)
     pl.semaphore_wait(barrier, T - 1 + O - 1)
 
-    def ag_right(s):
-        src = packed if s == 0 else right_in.at[s - 1]
-        return remote(src, right_in.at[s], agr_s.at[s], agr_r.at[s], right)
-
-    def ag_left(s):
-        src = packed if s == 0 else left_in.at[s - 1]
-        return remote(src, left_in.at[s], agl_s.at[s], agl_r.at[s], left)
-
-    ag_right(0).start()
-    ag_left(0).start()
+    def rightward(s, h):
+        return not (s == A - 1 and SUB == 2 and h == 1)
+
+    def leftward(s, h):
+        return s < A - 1 or (SUB == 2 and h == 1)
+
+    def ag(s, h, into, ssem, rsem, to):
+        src = packed.at[:, part(h)] if s == 0 else into.at[s - 1, :, part(h)]
+        at = s * SUB + h
+        return remote(src, into.at[s, :, part(h)], ssem.at[at], rsem.at[at], to)
+
+    def ag_right(s, h):
+        return ag(s, h, right_in, agr_s, agr_r, right)
+
+    def ag_left(s, h):
+        return ag(s, h, left_in, agl_s, agl_r, left)
+
+    for j in range(SUB):
+        if rightward(0, j):
+            ag_right(0, j).start()
+        if leftward(0, SUB - 1 - j):
+            ag_left(0, SUB - 1 - j).start()
     id_copies = [
         remote(ids_in, ids_all.at[k - 1], id_s.at[k - 1], id_r.at[k - 1], to_tm(k))
         for k in range(1, T)
@@ -191,21 +221,27 @@
 
     load(0).wait()
     obs = dot(packed[...], dv[0], NT)
-    ids = ids_in[0:1, :]
+    ids = ids_in[0:1, :].astype(jnp.float32)
     ca, ab, fwd, bwd = filters(ar_ref, ma_ref, aro_ref, mao_ref, ids, pt)
-    for s in range(right_n):
-        ag_right(s).wait_recv()
-        if s + 1 < right_n:
-            ag_right(s + 1).start()
-        if s < left_n:
-            ag_left(s).wait_recv()
-            if s + 1 < left_n:
-                ag_left(s + 1).start()
-        load(-(s + 1)).wait()
-        obs = obs + dot(right_in[s], dv[(-(s + 1)) % T], NT)
-        if s < left_n:
-            load(s + 1).wait()
-            obs = obs + dot(left_in[s], dv[s + 1], NT)
+    for s in range(A):
+        for j in range(SUB):
+            h, g = j, SUB - 1 - j
+            if rightward(s, h):
+                ag_right(s, h).wait_recv()
+                if s + 1 < A and rightward(s + 1, h):
+                    ag_right(s + 1, h).start()
+            if leftward(s, g):
+                ag_left(s, g).wait_recv()
+                if s + 1 < A and leftward(s + 1, g):
+                    ag_left(s + 1, g).start()
+            if j == 0:
+                load((-(s + 1)) % T if s < A - 1 else A).wait()
+                if s < A - 1:
+                    load(s + 1).wait()
+            if rightward(s, h):
+                obs = obs + dot(right_in[s, :, part(h)], dv[(-(s + 1)) % T, :, part(h)], NT)
+            if leftward(s, g):
+                obs = obs + dot(left_in[s, :, part(g)], dv[s + 1, :, part(g)], NT)
     obs_out[...] = obs
     ob_copies = [
         remote(obs_out, obs_in.at[k - 1], ob_s.at[k - 1], ob_r.at[k - 1], to_order(k))
@@ -219,17 +255,16 @@
     at_last = jnp.where(ids == last, 1.0, 0.0)
     head_map = spread(ca, at_first)
     tail_map = spread(ab, at_last)
-    head16 = tall(head_map, n)
-    tail16 = tall(tail_map, n)
-    zeros64 = jnp.zeros((n // 2, 3 * n), jnp.float32)
-    head_low = jnp.concatenate([zeros64, head16[: n // 2]], axis=0)
+    head_map = jnp.concatenate(
+        [dot(head_map[:, c * n : (c + 1) * n], pt[c], NT, HI) for c in range(3)], axis=1
+    )
+    state_map = jnp.concatenate([tall(tail_map, n // 2), tall(head_map, n // 2)], axis=0)
     for copy in id_copies:
         copy.wait_recv()
     ids_e = []
     for e in range(T):
-        slot = lax.rem(me - e + T - 1, T)
-        slot = jnp.minimum(slot, T - 2)
-        ids_e.append(jnp.where(me == e, ids, ids_all[slot][0:1, :]))
+        slot = jnp.minimum(lax.rem(me - e + T - 1, T), T - 2)
+        ids_e.append(jnp.where(me == e, ids, ids_all[slot].astype(jnp.float32)))
     firsts = [v[:, 0:1] for v in ids_e]
     lasts = [v[:, n - 1 : n] for v in ids_e]
     runs = jnp.concatenate(
@@ -242,12 +277,9 @@
         copy.wait_recv()
     for k in range(1, O):
         obs = obs + obs_in[k - 1]
-    gaps3 = jnp.concatenate([gaps[0:1, :]] * 3, axis=1)
+    gaps3 = jnp.concatenate([gaps_in[0:1, :].astype(jnp.float32)] * 3, axis=1)
     masked = obs * gaps3
-    local = jnp.concatenate(
-        [dot(masked[:, c * n : (c + 1) * n], pt[c], NN, HI) for c in range(3)], axis=1
-    )
-    summary = dot(masked, tail16, NT, HI) + dot(local, head_low, NT, HI)
+    summary = dot(masked, state_map, NT, HI)
     summ_out[...] = summary
     su_copies = [
         remote(summ_out, summ_in.at[k - 1], su_s.at[k - 1], su_r.at[k - 1], to_tm(k))
@@ -256,8 +288,25 @@
     for copy in su_copies:
         copy.start()
     local_back = jnp.concatenate(
-        [dot(local[:, c * n : (c + 1) * n], pt[c], NT, HI) for c in range(3)], axis=1
-    )
+        [
+            dot(dot(masked[:, c * n : (c + 1) * n], pt[c], NN, HI), pt[c], NT, HI)
+            for c in range(3)
+        ],
+        axis=1,
+    )
+
+    def preconditioned(v, cols):
+        out = []
+        for m in range(cols.start // 128, cols.stop // 128):
+            x = v[:, m * 128 - cols.start : (m + 1) * 128 - cols.start]
+            top = x.astype(jnp.bfloat16)
+            rest = (x - top.astype(jnp.float32)).astype(jnp.bfloat16)
+            both = dot(jnp.concatenate([top, rest], axis=0), high[m], NT)
+            out.append(both[:rhs] + both[rhs:] + dot(top, low[m], NT))
+        return jnp.concatenate(out, axis=1)
+
+    get_res.wait()
+    applied[...] = preconditioned(res[...], slice(0, share))
     for copy in su_copies:
         copy.wait_recv()
     sums = []
@@ -283,55 +332,66 @@
         )
         mine_back = jnp.where(me == e - 1, back, mine_back)
     lane = lax.broadcasted_iota(jnp.int32, summary.shape, 1)
-    mine_in = jnp.where(lane < 3 * LAGS, mine_in, 0.0)
-    mine_back = jnp.where(lane < 3 * LAGS, mine_back, 0.0)
-    entered = dot(mine_in, head16, NN, HI)
-    entered_back = jnp.concatenate(
-        [dot(entered[:, c * n : (c + 1) * n], pt[c], NT, HI) for c in range(3)], axis=1
-    )
-    adjoint = local_back + entered_back + dot(mine_back, tail16, NN, HI)
+    states = jnp.where(lane < n // 2, mine_back, pltpu.roll(mine_in, n // 2, 1))
+    adjoint = local_back + dot(states, state_map, NN, HI)
     weighted = (adjoint * gaps3).astype(jnp.bfloat16)
 
-    def grad(dist):
-        return dot(weighted, dv[dist % T], NN)
-
-    def rs_right(s):
-        return remote(rs_right_out.at[s], rs_right_in.at[s], rr_s.at[s], rr_r.at[s], right)
-
-    def rs_left(s):
-        return remote(rs_left_out.at[s], rs_left_in.at[s], rl_s.at[s], rl_r.at[s], left)
-
-    for s in range(right_n):
-        piece = grad(right_n - s)
-        if s > 0:
-            rs_right(s - 1).wait_recv()
-            piece = piece + rs_right_in[s - 1].astype(jnp.float32)
-        rs_right_out[s] = piece.astype(LINK)
-        rs_right(s).start()
-        if s < left_n:
-            piece = grad(s - left_n)
-            if s > 0:
-                rs_left(s - 1).wait_recv()
-                piece = piece + rs_left_in[s - 1].astype(jnp.float32)
-            rs_left_out[s] = piece.astype(LINK)
-            rs_left(s).start()
-    own = grad(0)
-    blocks = precond.shape[0]
-    for m in range(blocks):
-        cols = slice(m * 128, (m + 1) * 128)
-        applied[:, cols] = dot(res[:, cols], precond[m], NT, HI)
-    rs_right(right_n - 1).wait_recv()
-    own = own + rs_right_in[right_n - 1].astype(jnp.float32)
-    if left_n > 0:
-        rs_left(left_n - 1).wait_recv()
-        own = own + rs_left_in[left_n - 1].astype(jnp.float32)
-    image = own + kaula[...] * direc[...]
-    for m in range(blocks):
-        cols = slice(m * 128, (m + 1) * 128)
-        image_applied[:, cols] = dot(image[:, cols], precond[m], NT, HI)
+    def grad(dist, h):
+        return dot(weighted, dv[dist % T, :, part(h)], NN)
+
+    def rs_right(s, h):
+        at = s * SUB + h
+        return remote(
+            rs_right_out.at[s, :, part(h)], rs_right_in.at[s, :, part(h)],
+            rr_s.at[at], rr_r.at[at], right,
+        )
+
+    def rs_left(s, h):
+        at = s * SUB + h
+        return remote(
+            rs_left_out.at[s, :, part(h)], rs_left_in.at[s, :, part(h)],
+            rl_s.at[at], rl_r.at[at], left,
+        )
+
+    def sends_right(s, h):
+        return rightward(A - 1 - s, h)
+
+    def sends_left(s, h):
+        return leftward(A - 1 - s, h)
+
+    for s in range(A):
+        for j in range(SUB):
+            h, g = j, SUB - 1 - j
+            if sends_right(s, h):
+                piece = grad(A - s, h)
+                if s > 0 and sends_right(s - 1, h):
+                    rs_right(s - 1, h).wait_recv()
+                    piece = piece + rs_right_in[s - 1, :, part(h)].astype(jnp.float32)
+                rs_right_out[s, :, part(h)] = piece.astype(LINK)
+                rs_right(s, h).start()
+            if sends_left(s, g):
+                piece = grad(s - A, g)
+                if s > 0 and sends_left(s - 1, g):
+                    rs_left(s - 1, g).wait_recv()
+                    piece = piece + rs_left_in[s - 1, :, part(g)].astype(jnp.float32)
+                rs_left_out[s, :, part(g)] = piece.astype(LINK)
+                rs_left(s, g).start()
+    owns = [grad(0, h) for h in range(SUB)]
+    images = []
+    for h in range(SUB):
+        own = owns[h] + kaula[:, part(h)] * direc[:, part(h)]
+        if sends_right(A - 1, h):
+            rs_right(A - 1, h).wait_recv()
+            own = own + rs_right_in[A - 1, :, part(h)].astype(jnp.float32)
+        if sends_left(A - 1, h):
+            rs_left(A - 1, h).wait_recv()
+            own = own + rs_left_in[A - 1, :, part(h)].astype(jnp.float32)
+        images.append(own)
+        image_applied[:, part(h)] = preconditioned(own, part(h))
+    image = jnp.concatenate(images, axis=1)
+    image_out[...] = image
     app, imapp = applied[...], image_applied[...]
     d, r = direc[...], res[...]
-    rhs = d.shape[0]
     lane = lax.broadcasted_iota(jnp.int32, (rhs, 128), 1)
     row = lax.broadcasted_iota(jnp.int32, (rhs, 128), 0)
     products = [r * app, d * image, image * app, image * imapp]
@@ -362,18 +422,44 @@
     ]
     step = old_rz / curvature
     new_rz = old_rz - 2.0 * step * cross + step * step * quad
-    new_sol[...] = sol[...] + step * d
-    new_res[...] = r - step * image
-    new_dir[...] = app - step * imapp + (new_rz / old_rz) * d
-
-    for s in range(right_n):
-        ag_right(s).wait_send()
-        rs_right(s).wait_send()
-    for s in range(left_n):
-        ag_left(s).wait_send()
-        rs_left(s).wait_send()
+    comb_out[...] = app - step * imapp
+    scal_out[...] = jnp.where(lane == 0, step, new_rz / old_rz)
+
+    for s in range(A):
+        for h in range(SUB):
+            if rightward(s, h):
+                ag_right(s, h).wait_send()
+            if leftward(s, h):
+                ag_left(s, h).wait_send()
+            if sends_right(s, h):
+                rs_right(s, h).wait_send()
+            if sends_left(s, h):
+                rs_left(s, h).wait_send()
     for copy in id_copies + ob_copies + su_copies + c1 + c2:
         copy.wait_send()
+
+
+def finish(image, comb, scal, sol, res, direc, new_sol, new_res, new_dir, got, put, isem, osem):
+    def fetch(k, ref):
+        return pltpu.make_async_copy(ref.at[:, 0, :], got.at[k], isem.at[k])
+
+    def store(k, ref):
+        return pltpu.make_async_copy(put.at[k], ref.at[:, 0, :], osem.at[k])
+
+    for k, ref in ((2, direc), (0, sol), (1, res)):
+        fetch(k, ref).start()
+    step, ratio = scal[:, 0:1], scal[:, 1:2]
+    fetch(2, direc).wait()
+    put[2] = comb[...] + ratio * got[2]
+    store(2, new_dir).start()
+    fetch(0, sol).wait()
+    put[0] = got[0] + step * got[2]
+    store(0, new_sol).start()
+    fetch(1, res).wait()
+    put[1] = got[1] - step * image[...]
+    store(1, new_res).start()
+    for k, ref in ((2, new_dir), (0, new_sol), (1, new_res)):
+        store(k, ref).wait()
 
 
 def on_device(
@@ -384,42 +470,52 @@
     columns = design.shape[2]
     share = direction.shape[2]
     rhs = direction.shape[0]
+    blocks = precond.shape[1]
     f32, bf16 = jnp.float32, jnp.bfloat16
-    flat = lambda v: v.reshape(rhs, share)
-    ids8 = jnp.broadcast_to(segment_ids.astype(f32)[None, :], (8, n))
-    gaps8 = jnp.broadcast_to(gap_flags.astype(f32)[None, :], (8, n))
-    packed = flat(direction).astype(bf16)
-    right_n, left_n = T // 2, T - 1 - T // 2
+    SUB = 2 if share % 256 == 0 else 1
+    A = T // 2
     vmem = pl.BlockSpec(memory_space=pltpu.VMEM)
     smem = pl.BlockSpec(memory_space=pltpu.SMEM)
+    hbm = pl.BlockSpec(memory_space=pl.ANY)
     V, D = pltpu.VMEM, lambda k: pltpu.SemaphoreType.DMA((max(k, 1),))
-    L = max(left_n, 1)
-    outs = pl.pallas_call(
-        functools.partial(kernel, T, O),
-        out_shape=[jax.ShapeDtypeStruct((rhs, share), f32)] * 3,
-        in_specs=[pl.BlockSpec(memory_space=pl.ANY), vmem, vmem, vmem, smem, smem, smem, smem,
-                  vmem, vmem, vmem, vmem, vmem],
+    vec = jax.ShapeDtypeStruct((rhs, share), f32)
+    image, comb, scal = pl.pallas_call(
+        functools.partial(kernel, T, O, SUB),
+        out_shape=[vec, vec, jax.ShapeDtypeStruct((rhs, 128), f32)],
+        in_specs=[hbm, vmem, vmem, smem, smem, smem, smem, vmem, hbm, hbm, hbm],
         out_specs=[vmem] * 3,
         scratch_shapes=[
-            V((T, 3 * n, share), bf16), V((right_n, rhs, share), bf16), V((L, rhs, share), bf16),
-            V((rhs, 3 * n), f32), V((O - 1, rhs, 3 * n), f32), V((T - 1, 8, n), f32),
+            V((T, 3 * n, share), bf16), V((blocks, 128, 128), f32), V((rhs, share), f32),
+            V((rhs, share), f32), V((rhs, share), bf16), V((blocks, 128, 128), bf16),
+            V((blocks, 128, 128), bf16),
+            V((A, rhs, share), bf16), V((A, rhs, share), bf16),
+            V((rhs, 3 * n), f32), V((O - 1, rhs, 3 * n), f32), V((T - 1, 1, n), jnp.int32),
             V((rhs, n), f32), V((T - 1, rhs, n), f32), V((3, n, n), f32),
-            V((right_n, rhs, share), LINK), V((L, rhs, share), LINK),
-            V((right_n, rhs, share), LINK), V((L, rhs, share), LINK),
+            V((A, rhs, share), LINK), V((A, rhs, share), LINK),
+            V((A, rhs, share), LINK), V((A, rhs, share), LINK),
             V((rhs, share), f32), V((rhs, share), f32),
             V((8, 128), f32), V((O - 1, 8, 128), f32), V((8, 128), f32), V((T - 1, 8, 128), f32),
-            D(T), D(right_n), D(right_n), D(L), D(L), D(O - 1), D(O - 1), D(T - 1), D(T - 1),
-            D(T - 1), D(T - 1), D(right_n), D(right_n), D(L), D(L), D(O - 1), D(O - 1),
-            D(T - 1), D(T - 1),
+            D(T), D(3), D(A * SUB), D(A * SUB), D(A * SUB), D(A * SUB), D(O - 1), D(O - 1),
+            D(T - 1), D(T - 1), D(T - 1), D(T - 1), D(A * SUB), D(A * SUB), D(A * SUB),
+            D(A * SUB), D(O - 1), D(O - 1), D(T - 1), D(T - 1),
         ],
         compiler_params=pltpu.CompilerParams(
             collective_id=0, has_side_effects=True, vmem_limit_bytes=56 * 1024 * 1024
         ),
     )(
-        design.reshape(3 * n, columns), packed, ids8, gaps8, ar_roots, ma_roots, ar_order,
-        ma_order, kaula, precond[0], flat(solution), flat(residual), flat(direction),
-    )
-    return tuple(v.reshape(direction.shape) for v in outs)
+        design.reshape(3 * n, columns), segment_ids.reshape(1, n), gap_flags.reshape(1, n),
+        ar_roots, ma_roots, ar_order, ma_order, kaula, precond[0], residual, direction,
+    )
+    full = jax.ShapeDtypeStruct(direction.shape, f32)
+    return tuple(
+        pl.pallas_call(
+            finish,
+            out_shape=[full] * 3,
+            in_specs=[vmem, vmem, vmem, hbm, hbm, hbm],
+            out_specs=[hbm] * 3,
+            scratch_shapes=[V((3, rhs, share), f32), V((3, rhs, share), f32), D(3), D(3)],
+        )(image, comb, scal, solution, residual, direction)
+    )
 
 
 def solution(mesh):

time: 74.3 us -> 56.5 us (0.76)
  local copies, waits for them, and re-layouts: 11.2 us -> 0 us
  Pallas kernels: 60.9 us -> 55.7 us
  other arithmetic: 1.32 us -> 0 us
    unnamed x6 -> x0, local copies, waits for them, and re-layouts: 9.99 us -> none
    pallas_call x1 -> x2, Pallas kernels: 60.9 us -> 55.7 us  [the longest x1 52.9 us: on_device(): pl.pallas_call(functools.partial(kernel, T, O, SUB), out_shape=[vec, vec,...]
    convert_element_type x2 -> x0, other arithmetic: 1.32 us -> none  [the longest x1 0.66 us: on_device(): gaps8 = jnp.broadcast_to(gap_flags.astype(f32)[None, :], (8, n))]
    broadcast_in_dim x2 -> x0, local copies, waits for them, and re-layouts: 1.18 us -> none  [the longest x1 0.6 us: on_device(): ids8 = jnp.broadcast_to(segment_ids.astype(f32)[None, :], (8, n))]
where the time goes in v2:
time: 56.5 us; the launch traced here: 56.3 us
  Pallas kernels  55.7 us (99%)
  between operations  0.64 us (1%)
    pallas_call x1, Pallas kernels, on_device(): pl.pallas_call(functools.partial(kernel, T, O, SUB), out_shape=[vec, vec,...  52.9 us
    pallas_call x1, Pallas kernels, on_device(): pl.pallas_call(finish, out_shape=[full] * 3, in_specs=[vmem, vmem, vmem,...  2.79 us

profile of v2, /device:TPU:0, one launch (start us, length us, event | category | flops | bytes accessed | tf_op | source)
XLA Modules:
  0.0 56.3 jit_solution(12525492343380059500)
XLA Ops:
  0.6 52.9 %shard_map.139 = (f32[16,2048]{1,0:T(8,128)}, f32[16,2048]{1,0:T(8,128)}, f32[16,128]{1,0:T(8,128)}) custom-call(bf16[384,16384]{1,0:T(8,128)(2,1)} %bitcast.4, s32[1,128]{1,0:T(1,128)} %bitcast.6, s32[1,128]{1,0:T(1,128)} %bitcast.7, f32[3,4]{1,0:T(4,128)} %ar_ref.1, f32[3,4]{1,0:T(4,128)} %ma_ref.1, s32[3]{0:T(128)} %aro_ref.1, s32[3]{0:T(128)} %mao_ref.1, ...), custom_call_target="tpu_custom_call" | custom-call | tf_op jit(solution)/shard_map/pallas_call | solution.py:482
  53.5 2.8 %shard_map.140 = (f32[16,1,2048]{2,1,0:T(1,128)}, f32[16,1,2048]{2,1,0:T(1,128)}, f32[16,1,2048]{2,1,0:T(1,128)}) custom-call(f32[16,2048]{1,0:T(8,128)} %get-tuple-element.6.image, f32[16,2048]{1,0:T(8,128)} %get-tuple-element.7.comb, f32[16,128]{1,0:T(8,128)} %get-tuple-element.8.scal, f32[16,1,2048]{2,1,0:T(1,128)} %sol.1, f32[16,1,2048]{2,1,0:T(1,128)} %res.1, ...), custom_call_target="tpu_custom_call" | custom-call | tf_op jit(solution)/shard_map/pallas_call | solution.py:511
